TPU v7x, 32 devices: a whole 2x2x4 slice. The times are simulated.
32 devices in a mesh: dp: 8 (over z, core), tensor: 4 (over y, x).
Axes of the slice: x: 2, y: 2, z: 4, core: 2. Of those that a mesh axis runs over, the one named last changes fastest.
Arguments:
- byte_in: bfloat16 [32, 4096, 768], P('dp', 'tensor'), may hold values from -6 to 6
- lengths: int32 [32], P('dp'), may hold values from 1024 to 4096, as said below
- latent: bfloat16 [256, 1280], P('tensor', 'dp'), may hold values from -6 to 6
- g_in: float32 [768], replicated, may hold values from 0.1 to 1.9
- b_in: float32 [768], replicated, may hold values from -3 to 3
- g_lat: float32 [1280], replicated, may hold values from 0.1 to 1.9
- b_lat: float32 [1280], replicated, may hold values from -3 to 3
- w_query: bfloat16 [1280, 256], P('dp', 'tensor'), may hold values from -0.15625 to 0.15625
- w_key: bfloat16 [768, 256], P('dp', 'tensor'), may hold values from -0.21875 to 0.21875
- w_value: bfloat16 [768, 1280], P('dp', 'tensor'), may hold values from -0.21875 to 0.21875
- w_out: bfloat16 [1280, 1280], P('tensor', 'dp'), may hold values from -6 to 6
- g_mlp: float32 [1280], replicated, may hold values from 0.1 to 1.9
- b_mlp: float32 [1280], replicated, may hold values from -3 to 3
- w_hidden: bfloat16 [1280, 1280], P('dp', 'tensor'), may hold values from -0.15625 to 0.15625
- b_hidden: float32 [1280], replicated, may hold values from -3 to 3
- w_back: bfloat16 [1280, 1280], P('tensor', 'dp'), may hold values from -0.15625 to 0.15625
- b_back: float32 [1280], replicated, may hold values from -3 to 3
- cotangent: float32 [32, 256, 1280], P('dp', 'tensor'), may hold values from -6 to 6
Outputs:
- latents_out: float32 [32, 256, 1280], P('dp', 'tensor')
- grad_bytes: float32 [32, 4096, 768], P('dp', 'tensor')
- grad_latent: float32 [256, 1280], P('tensor', 'dp')
- grad_g_in: float32 [768], replicated
- grad_b_in: float32 [768], replicated
- grad_g_lat: float32 [1280], replicated
- grad_b_lat: float32 [1280], replicated
- grad_w_query: float32 [1280, 256], P('dp', 'tensor')
- grad_w_key: float32 [768, 256], P('dp', 'tensor')
- grad_w_value: float32 [768, 1280], P('dp', 'tensor')
- grad_w_out: float32 [1280, 1280], P('tensor', 'dp')
- grad_g_mlp: float32 [1280], replicated
- grad_b_mlp: float32 [1280], replicated
- grad_w_hidden: float32 [1280, 1280], P('dp', 'tensor')
- grad_b_hidden: float32 [1280], replicated
- grad_w_back: float32 [1280, 1280], P('tensor', 'dp')
- grad_b_back: float32 [1280], replicated
Inputs may be any that keep to these rules, and one draw needn't show every extreme that they name: Sequence b has live bytes at slots below lengths[b] and padding from there on; the first sequence is full.
All inputs are finite; a program needn't handle non-finite values.
Results may differ from a plain program's by a relative error of at most 0.019.
Values may be sent and summed in bfloat16 or wider, within the bound.
No kernel may reach another device: no remote copies, remote signals or barrier semaphores. Data moves between devices by JAX's collectives and lax.ppermute only.
A program may use at most 256 MiB of HBM per device.

v0:
```python
from functools import partial
import jax
import jax.numpy as jnp
from jax import lax
from jax.sharding import PartitionSpec as P

HQ = 32
HV = 160
NEGATIVE = -1e30


def normalize(values, gain, shift):
    center = jnp.mean(values, axis=-1, keepdims=True)
    centered = values - center
    spread = jnp.mean(centered * centered, axis=-1, keepdims=True)
    return centered * lax.rsqrt(spread + 1e-05) * gain + shift


def norm_backward(values, gain, shift, upstream):
    normed, pullback = jax.vjp(normalize, values, gain, shift)
    return pullback(upstream)


def exact_gelu(values):
    return jax.nn.gelu(values, approximate=False)


def head_scores(query_all, keys_seq, length):
    heads = query_all.shape[1] // HQ
    query_heads = query_all.reshape(query_all.shape[0], heads, HQ)
    key_heads = keys_seq.reshape(keys_seq.shape[0], heads, HQ)
    raw = jnp.einsum("nhd,lhd->hnl", query_heads, key_heads, preferred_element_type=jnp.float32)
    live = lax.iota(jnp.int32, keys_seq.shape[0]) < length
    return jnp.where(live[None, None, :], raw * HQ ** (-0.5), NEGATIVE)


def attend_forward(query_all, item):
    keys_seq, values_seq, length = item
    scores = head_scores(query_all, keys_seq, length)
    summit = jnp.max(scores, axis=-1, keepdims=True)
    weights = jnp.exp(scores - summit)
    total = jnp.sum(weights, axis=-1, keepdims=True)
    probs = weights / total
    heads = scores.shape[0]
    value_heads = values_seq.reshape(values_seq.shape[0], heads, HV)
    mixed = jnp.einsum(
        "hnl,lhe->nhe", probs.astype(jnp.bfloat16), value_heads, preferred_element_type=jnp.float32
    )
    mixed = mixed.reshape(mixed.shape[0], heads * HV).astype(jnp.bfloat16)
    return (mixed, (summit + jnp.log(total))[..., 0])


def score_backward(query_all, keys_seq, values_seq, probs, grad_mixed, inner):
    heads = probs.shape[0]
    latents = query_all.shape[0]
    slots = keys_seq.shape[0]
    value_heads = values_seq.reshape(slots, heads, HV)
    grad_heads = grad_mixed.reshape(latents, heads, HV)
    grad_probs = jnp.einsum(
        "nhe,lhe->hnl", grad_heads, value_heads, preferred_element_type=jnp.float32
    )
    grad_values = jnp.einsum(
        "hnl,nhe->lhe", probs.astype(jnp.bfloat16), grad_heads, preferred_element_type=jnp.float32
    )
    inner = jnp.sum(probs * grad_probs, axis=-1, keepdims=True)
    grad_scores = (probs * (grad_probs - inner) * HQ ** (-0.5)).astype(jnp.bfloat16)
    query_heads = query_all.reshape(latents, heads, HQ)
    key_heads = keys_seq.reshape(slots, heads, HQ)
    grad_query = jnp.einsum(
        "hnl,lhd->nhd", grad_scores, key_heads, preferred_element_type=jnp.float32
    )
    grad_keys = jnp.einsum(
        "hnl,nhd->lhd", grad_scores, query_heads, preferred_element_type=jnp.float32
    )
    return (
        grad_query.reshape(latents, heads * HQ),
        grad_keys.reshape(slots, heads * HQ).astype(jnp.bfloat16),
        grad_values.reshape(slots, heads * HV).astype(jnp.bfloat16),
    )


def rows_backward(query_all, item):
    keys_seq, values_seq, length, log_total, grad_mixed = item
    scores = head_scores(query_all, keys_seq, length)
    probs = jnp.exp(scores - log_total[..., None])
    return score_backward(query_all, keys_seq, values_seq, probs, grad_mixed, None)


def on_device(
    byte_in,
    lengths,
    latent,
    g_in,
    b_in,
    g_lat,
    b_lat,
    w_query,
    w_key,
    w_value,
    w_out,
    g_mlp,
    b_mlp,
    w_hidden,
    b_hidden,
    w_back,
    b_back,
    cotangent,
):
    full_query, full_key, full_value, full_hidden, full_out, full_back, latent_rows = (
        lax.all_gather(w_query, "dp", axis=0, tiled=True),
        lax.all_gather(w_key, "dp", axis=0, tiled=True),
        lax.all_gather(w_value, "dp", axis=0, tiled=True),
        lax.all_gather(w_hidden, "dp", axis=0, tiled=True),
        lax.all_gather(w_out, "dp", axis=1, tiled=True),
        lax.all_gather(w_back, "dp", axis=1, tiled=True),
        lax.all_gather(latent, "dp", axis=1, tiled=True),
    )
    tensor_rank = lax.axis_index("tensor")
    latent_float = latent_rows.astype(jnp.float32)
    latent_norm = normalize(latent_float, g_lat, b_lat).astype(jnp.bfloat16)
    byte_float = byte_in.astype(jnp.float32)
    byte_norm = normalize(byte_float, g_in, b_in).astype(jnp.bfloat16)
    latent_all, byte_all = (
        lax.all_gather(latent_norm, "tensor", axis=0, tiled=True),
        lax.all_gather(byte_norm, "tensor", axis=1, tiled=True),
    )
    keys = jnp.einsum("slc,cq->slq", byte_all, full_key, preferred_element_type=jnp.float32).astype(
        jnp.bfloat16
    )
    values = jnp.einsum(
        "slc,cv->slv", byte_all, full_value, preferred_element_type=jnp.float32
    ).astype(jnp.bfloat16)
    query = jnp.dot(latent_all, full_query, preferred_element_type=jnp.float32).astype(jnp.bfloat16)
    mixed, log_totals = lax.map(partial(attend_forward, query), (keys, values, lengths))
    attn_term = jnp.einsum("snv,vd->snd", mixed, full_out, preferred_element_type=jnp.float32)
    attn_rows = lax.psum_scatter(attn_term, "tensor", scatter_dimension=1, tiled=True)
    middle = latent_float[None] + attn_rows
    hidden_norm = normalize(middle, g_mlp, b_mlp).astype(jnp.bfloat16)
    out_grad = cotangent.astype(jnp.bfloat16)
    hidden_all, out_grad_all = (
        lax.all_gather(hidden_norm, "tensor", axis=1, tiled=True),
        lax.all_gather(out_grad, "tensor", axis=1, tiled=True),
    )
    width = full_hidden.shape[1]
    offset = tensor_rank * width
    bias_part = lax.dynamic_slice_in_dim(b_hidden, offset, width)
    pre = (
        jnp.einsum("snd,df->snf", hidden_all, full_hidden, preferred_element_type=jnp.float32)
        + bias_part
    )
    activation, gelu_pull = jax.vjp(exact_gelu, pre)
    act_low = activation.astype(jnp.bfloat16)
    branch_term = jnp.einsum("snf,fd->snd", act_low, full_back, preferred_element_type=jnp.float32)
    branch_rows = lax.psum_scatter(
        branch_term.astype(jnp.bfloat16), "tensor", scatter_dimension=1, tiled=True
    ).astype(jnp.float32)
    latents_out = middle + branch_rows + b_back
    grad_back_part = jnp.einsum(
        "snf,snd->fd", act_low, out_grad_all, preferred_element_type=jnp.float32
    )
    grad_act = jnp.einsum(
        "snd,fd->snf", out_grad_all, full_back, preferred_element_type=jnp.float32
    )
    grad_pre = gelu_pull(grad_act)[0].astype(jnp.bfloat16)
    grad_bias_part = jnp.sum(grad_pre.astype(jnp.float32), axis=(0, 1))
    grad_hidden_part = jnp.einsum(
        "snd,snf->df", hidden_all, grad_pre, preferred_element_type=jnp.float32
    )
    hidden_term = jnp.einsum(
        "snf,df->snd", grad_pre, full_hidden, preferred_element_type=jnp.float32
    )
    grad_hidden = lax.psum_scatter(hidden_term, "tensor", scatter_dimension=1, tiled=True)
    grad_mid_norm, grad_g_mlp, grad_b_mlp = norm_backward(middle, g_mlp, b_mlp, grad_hidden)
    grad_middle = cotangent + grad_mid_norm
    middle_low = grad_middle.astype(jnp.bfloat16)
    middle_all = lax.all_gather(middle_low, "tensor", axis=1, tiled=True)
    grad_out_part = jnp.einsum("snv,snd->vd", mixed, middle_all, preferred_element_type=jnp.float32)
    grad_mixed = jnp.einsum(
        "snd,vd->snv", middle_all, full_out, preferred_element_type=jnp.float32
    ).astype(jnp.bfloat16)
    query_parts, grad_keys, grad_values = lax.map(
        partial(rows_backward, query), (keys, values, lengths, log_totals, grad_mixed)
    )
    grad_query = query_parts.astype(jnp.bfloat16)
    grad_query_part = jnp.einsum(
        "nd,snq->dq", latent_all, grad_query, preferred_element_type=jnp.float32
    )
    latent_term = jnp.einsum(
        "snq,dq->nd", grad_query, full_query, preferred_element_type=jnp.float32
    )
    grad_key_part = jnp.einsum(
        "slc,slq->cq", byte_all, grad_keys, preferred_element_type=jnp.float32
    )
    grad_value_part = jnp.einsum(
        "slc,slv->cv", byte_all, grad_values, preferred_element_type=jnp.float32
    )
    byte_term = jnp.einsum("slq,cq->slc", grad_keys, full_key, preferred_element_type=jnp.float32)
    byte_term = byte_term + jnp.einsum(
        "slv,cv->slc", grad_values, full_value, preferred_element_type=jnp.float32
    )
    grad_latent_norm, grad_byte_norm = (
        lax.psum_scatter(
            latent_term.astype(jnp.bfloat16), "tensor", scatter_dimension=0, tiled=True
        ).astype(jnp.float32),
        lax.psum_scatter(
            byte_term.astype(jnp.bfloat16), "tensor", scatter_dimension=1, tiled=True
        ).astype(jnp.float32),
    )
    grad_bytes, grad_g_in, grad_b_in = norm_backward(byte_float, g_in, b_in, grad_byte_norm)
    grad_lat_rows, grad_g_lat, grad_b_lat = norm_backward(
        latent_float, g_lat, b_lat, grad_latent_norm
    )
    latent_part = grad_lat_rows + jnp.sum(grad_middle, axis=0)
    grad_w_query, grad_w_key, grad_w_value, grad_w_hidden, grad_w_out, grad_w_back, grad_latent = (
        lax.psum_scatter(
            grad_query_part.astype(jnp.bfloat16), "dp", scatter_dimension=0, tiled=True
        ).astype(jnp.float32),
        lax.psum_scatter(
            grad_key_part.astype(jnp.bfloat16), "dp", scatter_dimension=0, tiled=True
        ).astype(jnp.float32),
        lax.psum_scatter(
            grad_value_part.astype(jnp.bfloat16), "dp", scatter_dimension=0, tiled=True
        ).astype(jnp.float32),
        lax.psum_scatter(
            grad_hidden_part.astype(jnp.bfloat16), "dp", scatter_dimension=0, tiled=True
        ).astype(jnp.float32),
        lax.psum_scatter(
            grad_out_part.astype(jnp.bfloat16), "dp", scatter_dimension=1, tiled=True
        ).astype(jnp.float32),
        lax.psum_scatter(
            grad_back_part.astype(jnp.bfloat16), "dp", scatter_dimension=1, tiled=True
        ).astype(jnp.float32),
        lax.psum_scatter(
            latent_part.astype(jnp.bfloat16), "dp", scatter_dimension=1, tiled=True
        ).astype(jnp.float32),
    )
    bias_full = lax.dynamic_update_slice_in_dim(
        jnp.zeros(b_hidden.shape, jnp.float32), grad_bias_part, offset, 0
    )
    back_bias = jnp.sum(cotangent, axis=(0, 1))
    (
        sum_g_in,
        sum_b_in,
        sum_g_lat,
        sum_b_lat,
        sum_g_mlp,
        sum_b_mlp,
        sum_hidden_bias,
        sum_back_bias,
    ) = lax.psum(
        (
            grad_g_in,
            grad_b_in,
            grad_g_lat,
            grad_b_lat,
            grad_g_mlp,
            grad_b_mlp,
            bias_full,
            back_bias,
        ),
        ("dp", "tensor"),
    )
    return (
        latents_out,
        grad_bytes,
        grad_latent,
        sum_g_in,
        sum_b_in,
        sum_g_lat,
        sum_b_lat,
        grad_w_query,
        grad_w_key,
        grad_w_value,
        grad_w_out,
        sum_g_mlp,
        sum_b_mlp,
        grad_w_hidden,
        sum_hidden_bias,
        grad_w_back,
        sum_back_bias,
    )


def solution(mesh):
    return jax.shard_map(
        on_device,
        mesh=mesh,
        in_specs=(
            P("dp", "tensor", None),
            P("dp"),
            P("tensor", "dp"),
            P(),
            P(),
            P(),
            P(),
            P("dp", "tensor"),
            P("dp", "tensor"),
            P("dp", "tensor"),
            P("tensor", "dp"),
            P(),
            P(),
            P("dp", "tensor"),
            P(),
            P("tensor", "dp"),
            P(),
            P("dp", "tensor", None),
        ),
        out_specs=(
            P("dp", "tensor", None),
            P("dp", "tensor", None),
            P("tensor", "dp"),
            P(),
            P(),
            P(),
            P(),
            P("dp", "tensor"),
            P("dp", "tensor"),
            P("dp", "tensor"),
            P("tensor", "dp"),
            P(),
            P(),
            P("dp", "tensor"),
            P(),
            P("tensor", "dp"),
            P(),
        ),
        check_vma=False,
    )
```

profile of v0, /device:TPU:0, one launch (start us, length us, event | category | flops | bytes accessed | tf_op | source)
XLA Modules:
  0.0 1378.6 jit_solution(1738117160215363576)
XLA Ops:
  65.7 17.8 %all_gather.40 = bf16[256,1280]{1,0:T(8,128)(2,1)S(1)} all-gather(bf16[64,1280]{1,0:T(8,128)(2,1)S(1)} %add_convert_fusion.4), channel_id=1, replica_groups=mesh['dp'=8,'tensor'=4] {'tensor'}, dimensions={0}, use_global_device_ids=true | all-gather | bytes 819200 | tf_op jit(solution)/shard_map/all_gather | solution.py:124
  83.6 16.1 %all_gather.38 = bf16[768,320]{1,0:T(8,128)(2,1)} all-gather(bf16[96,320]{1,0:T(8,128)(2,1)S(1)} %copy-done.30), channel_id=1, replica_groups=mesh['dp'=8,'tensor'=4] {'dp'}, dimensions={0}, use_global_device_ids=true | all-gather | bytes 552960 | tf_op jit(solution)/shard_map/all_gather | solution.py:112
  100.0 17.1 %all_gather.42 = bf16[320,1280]{0,1:T(8,128)(2,1)S(1)} all-gather(bf16[320,160]{0,1:T(8,128)(2,1)S(1)} %copy-done.26), channel_id=1, replica_groups=mesh['dp'=8,'tensor'=4] {'dp'}, dimensions={1}, use_global_device_ids=true | all-gather | bytes 921600 | tf_op jit(solution)/shard_map/all_gather | solution.py:114
  117.1 137.7 %all-gather.8.cloned.1.call-done = bf16[4,4096,768]{2,1,0:T(8,128)(2,1)} async-done(((bf16[4,1024,768]{2,1,0:T(8,128)(2,1)}), bf16[4,4096,768]{2,1,0:T(8,128)(2,1)}) %all-gather.8.cloned.1.call-update) | async-done | bytes 25165840 | tf_op jit(solution)/shard_map/all_gather | solution.py:125
  254.8 15.8 %convolution_convert_fusion.3 = bf16[4,4096,64]{1,2,0:T(8,128)(2,1)S(1)} fusion(bf16[4,4096,768]{2,1,0:T(8,128)(2,1)} %all-gather.8.cloned.1.call-done, bf16[768,64,1]{0,1,2:T(8,128)(2,1)S(1)} %reshape.241), kind=kOutput, calls=%fused_computation.59 | convolution fusion | flops 1611661312 | bytes 27361280 | tf_op jit(solution)/shard_map/slc,cq->slq/dot_general | solution.py:127
  270.7 17.0 %convolution_convert_fusion.2 = bf16[4,4096,320]{1,2,0:T(8,128)(2,1)} fusion(bf16[4,4096,768]{2,1,0:T(8,128)(2,1)} %all-gather.8.cloned.1.call-done, bf16[768,320]{1,0:T(8,128)(2,1)S(1)} %copy-done.9), kind=kOutput, calls=%fused_computation.56 | convolution fusion | flops 8058306560 | bytes 36143104 | tf_op jit(solution)/shard_map/slc,cv->slv/dot_general | solution.py:130
  287.7 50.4 %while.26 = (s32[]{:T(128)}, bf16[4,256,320]{1,2,0:T(8,128)(2,1)}, f32[4,2,256]{2,1,0:T(2,128)S(1)}, bf16[4,4096,320]{1,2,0:T(8,128)(2,1)}, s32[4]{0:T(128)S(1)}...) while((s32[]{:T(128)}, bf16[4,256,320]{1,2,0:T(8,128)(2,1)}, ...), condition=%wide.region_7.8_spmd, body=%wide.region_4.7_spmd.sunk | while | flops 830557696 | bytes 35160188 | solution.py:134
  343.6 61.5 %reduce-scatter.19.cloned.1.call-done = f32[4,64,1280]{2,1,0:T(8,128)} async-done(((f32[4,256,1280]{2,1,0:T(8,128)}), f32[4,64,1280]{2,1,0:T(8,128)}) %reduce-scatter.19.cloned.1.call-update) | async-done | bytes 1310736 | tf_op jit(solution)/shard_map/reduce_scatter | solution.py:136
  410.2 17.2 %all_gather.44 = bf16[1280,320]{1,0:T(8,128)(2,1)} all-gather(bf16[160,320]{1,0:T(8,128)(2,1)S(1)} %copy-done.27), channel_id=1, replica_groups=mesh['dp'=8,'tensor'=4] {'dp'}, dimensions={0}, use_global_device_ids=true | all-gather | bytes 921600 | tf_op jit(solution)/shard_map/all_gather | solution.py:113
  427.3 17.5 %all_gather.45 = bf16[320,1280]{0,1:T(8,128)(2,1)} all-gather(bf16[320,160]{0,1:T(8,128)(2,1)S(1)} %copy-done.28), channel_id=1, replica_groups=mesh['dp'=8,'tensor'=4] {'dp'}, dimensions={1}, use_global_device_ids=true | all-gather | bytes 921600 | tf_op jit(solution)/shard_map/all_gather | solution.py:115
  456.6 32.9 %all-gather.12.cloned.1.call-done = bf16[4,256,1280]{2,1,0:T(8,128)(2,1)} async-done(((bf16[4,64,1280]{2,1,0:T(8,128)(2,1)}), bf16[4,256,1280]{2,1,0:T(8,128)(2,1)}) %all-gather.12.cloned.1.call-update) | async-done | bytes 2621456 | tf_op jit(solution)/shard_map/all_gather | solution.py:142
  503.8 57.0 %reduce-scatter.23.cloned.1.call-done = f32[4,64,1280]{2,1,0:T(8,128)} async-done(((f32[4,256,1280]{2,1,0:T(8,128)}), f32[4,64,1280]{2,1,0:T(8,128)}) %reduce-scatter.23.cloned.1.call-update) | async-done | bytes 1310736 | tf_op jit(solution)/shard_map/reduce_scatter | solution.py:172
  563.2 40.1 %reduce-scatter.21.cloned.1.call-done = bf16[4,64,1280]{2,1,0:T(8,128)(2,1)} async-done(((bf16[4,256,1280]{2,1,0:T(8,128)(2,1)}), bf16[4,64,1280]{2,1,0:T(8,128)(2,1)}) %reduce-scatter.21.cloned.1.call-update) | async-done | bytes 655376 | tf_op jit(solution)/shard_map/reduce_scatter | solution.py:154
  608.3 39.7 %all-gather.14.cloned.1.call-done = bf16[4,256,1280]{2,1,0:T(8,128)(2,1)} async-done(((bf16[4,64,1280]{2,1,0:T(8,128)(2,1)}), bf16[4,256,1280]{2,1,0:T(8,128)(2,1)}) %all-gather.14.cloned.1.call-update) | async-done | bytes 2621456 | tf_op jit(solution)/shard_map/all_gather | solution.py:176
  651.9 174.2 %while.27 = (s32[]{:T(128)}, bf16[4,256,64]{1,2,0:T(8,128)(2,1)S(1)}, bf16[4,4096,64]{1,2,0:T(8,128)(2,1)S(1)}, bf16[4,4096,320]{1,2,0:T(8,128)(2,1)}, bf16[4,40...) while((s32[]{:T(128)}, ...), condition=%wide.region_17.18_spmd, body=%wide.region_15.17_spmd.sunk | while | flops 1772368896 | bytes 112507056 | solution.py:181
  848.6 25.0 %fusion.47 = f32[4,4096,768]{2,1,0:T(8,128)} fusion(bf16[4,4096,320]{1,2,0:T(8,128)(2,1)} %get-tuple-element.112, bf16[768,320]{1,0:T(8,128)(2,1)S(1)} %copy-done.10), kind=kOutput, calls=%fused_computation.115 | convolution fusion | flops 8053063680 | bytes 61308928 | tf_op jit(solution)/shard_map/slv,cv->slc/dot_general | solution.py:198
  876.3 20.4 %fusion.31 = bf16[768,320]{1,0:T(8,128)(2,1)} fusion(bf16[4,4096,768]{2,1,0:T(8,128)(2,1)} %all-gather.8.cloned.1.call-done, bf16[4,4096,320]{1,2,0:T(8,128)(2,1)} %get-tuple-element.112), kind=kOutput, calls=%fused_computation.74 | convolution fusion | flops 8053309440 | bytes 36143104 | tf_op jit(solution)/shard_map/slc,slv->cv/dot_general | solution.py:194
  906.1 25.7 %add_convert_fusion = bf16[4,4096,768]{2,1,0:T(8,128)(2,1)} fusion(f32[4,4096,768]{2,1,0:T(8,128)} %fusion.47, bf16[4,4096,64]{1,2,0:T(8,128)(2,1)S(1)} %get-tuple-element.111, bf16[768,64,1]{0,1,2:T(8,128)(2,1)S(1)} %copy-done.16), kind=kOutput, calls=%fused_computation.38 | convolution fusion | flops 1635778560 | bytes 77692928 | tf_op jit(solution)/shard_map/slq,cq->slc/dot_general | solution.py:197
  953.0 29.3 %reduce-scatter.39.cloned.1.call-done = bf16[160,64]{1,0:T(8,128)(2,1)} async-done(((bf16[1280,64]{1,0:T(8,128)(2,1)}), bf16[160,64]{1,0:T(8,128)(2,1)}) %reduce-scatter.39.cloned.1.call-update) | async-done | bytes 20496
  983.8 30.2 %reduce-scatter.29.cloned.1.call-done = bf16[96,320]{1,0:T(8,128)(2,1)} async-done(((bf16[768,320]{1,0:T(8,128)(2,1)}), bf16[96,320]{1,0:T(8,128)(2,1)}) %reduce-scatter.29.cloned.1.call-update) | async-done | bytes 61456 | tf_op jit(solution)/shard_map/reduce_scatter | solution.py:221
  1015.6 29.3 %reduce-scatter.37.cloned.1.call-done = bf16[160,64]{1,0:T(8,128)(2,1)} async-done(((bf16[1280,64]{1,0:T(8,128)(2,1)}), bf16[160,64]{1,0:T(8,128)(2,1)}) %reduce-scatter.37.cloned.1.call-update) | async-done | bytes 20496
  1046.3 31.4 %reduce-scatter.31.cloned.1.call-done = bf16[320,160]{0,1:T(8,128)(2,1)} async-done(((bf16[320,1280]{0,1:T(8,128)(2,1)}), bf16[320,160]{0,1:T(8,128)(2,1)}) %reduce-scatter.31.cloned.1.call-update) | async-done | bytes 102416 | tf_op jit(solution)/shard_map/reduce_scatter | solution.py:227
  1079.3 222.0 %reduce-scatter.25.cloned.1.call-done = bf16[4,1024,768]{2,1,0:T(8,128)(2,1)} async-done(((bf16[4,4096,768]{2,1,0:T(8,128)(2,1)}), bf16[4,1024,768]{2,1,0:T(8,128)(2,1)}) %reduce-scatter.25.cloned.1.call-update) | async-done | bytes 6291472 | tf_op jit(solution)/shard_map/reduce_scatter | solution.py:205
  1318.3 40.9 %all-reduce = (f32[768]{0:T(1024)}, f32[768]{0:T(1024)}, f32[1280]{0:T(1024)}, f32[1280]{0:T(1024)}, f32[1280]{0:T(1024)}, /*index=5*/f32[1280]{0:T(1024)}, f32[1280]{0:T(1024)}, f32[1280]{0:T(1024)}) all-reduce(f32[768]{0:T(1024)S(1)} %get-tuple-element.114, ...), channel_id=1, replica_groups=mesh['dp'=8,'tensor'=4] {'dp','tensor'}, use_global_device_ids=true, to_apply=%region_28.29 | all-reduce | flops 9216 | bytes 73728 | tf_op jit(solution)/shard_map/psum | solution.py:250
  (309 shorter events, 421.6 us)
Async XLA Ops:
  7.2 247.6 %all-gather.8.cloned.1.call-start = ((), (), s32[]{:S(2)}) async-start(), calls=%async_computation.12 | async-start | bytes 31457280 | tf_op jit(solution)/shard_map/all_gather | solution.py:125
  19.3 385.8 %reduce-scatter.19.cloned.1.call-start = ((), (), s32[]{:S(2)}) async-start(), calls=%async_computation.13 | async-start | bytes 6553600 | tf_op jit(solution)/shard_map/reduce_scatter | solution.py:136
  35.9 218.9 %copy-start.15 = (bf16[768,64,1]{0,1,2:T(8,128)(2,1)}, bf16[768,64,1]{0,1,2:T(8,128)(2,1)S(1)}, u32[]{:S(2)}) copy-start(bf16[768,64,1]{0,1,2:T(8,128)(2,1)S(1)} %reshape.241) | copy-start | bytes 294916
  117.1 221.0 %copy-start.7 = (bf16[320,1280]{0,1:T(8,128)(2,1)}, bf16[320,1280]{0,1:T(8,128)(2,1)S(1)}, u32[]{:S(2)}) copy-start(bf16[320,1280]{0,1:T(8,128)(2,1)S(1)} %all_gather.42) | copy-start | bytes 2457604
  343.5 104.6 %all-gather.10.cloned.1.call-start = ((), (), s32[]{:S(2)}) async-start(), calls=%async_computation.14 | async-start | bytes 3276800 | tf_op jit(solution)/shard_map/all_gather | solution.py:141
  408.3 81.2 %all-gather.12.cloned.1.call-start = ((), (), s32[]{:S(2)}) async-start(), calls=%async_computation.16 | async-start | bytes 3276800 | tf_op jit(solution)/shard_map/all_gather | solution.py:142
  409.3 151.4 %reduce-scatter.23.cloned.1.call-start = ((), (), s32[]{:S(2)}) async-start(), calls=%async_computation.17 | async-start | bytes 6553600 | tf_op jit(solution)/shard_map/reduce_scatter | solution.py:172
  499.2 104.0 %reduce-scatter.21.cloned.1.call-start = ((), (), s32[]{:S(2)}) async-start(), calls=%async_computation.15 | async-start | bytes 3276800 | tf_op jit(solution)/shard_map/reduce_scatter | solution.py:154
  503.8 99.5 %copy-start.43 = (f32[1280]{0:T(1024)S(1)}, f32[1280]{0:T(1024)}, u32[]{:S(2)}) copy-start(f32[1280]{0:T(1024)} %param.38) | copy-start | bytes 15364
  503.8 144.2 %all-gather.14.cloned.1.call-start = ((), (), s32[]{:S(2)}) async-start(), calls=%async_computation.18 | async-start | bytes 3276800 | tf_op jit(solution)/shard_map/all_gather | solution.py:176
  608.2 288.6 %reduce-scatter.27.cloned.1.call-start = ((), (), s32[]{:S(2)}) async-start(), calls=%async_computation.20 | async-start | bytes 819200 | tf_op jit(solution)/shard_map/reduce_scatter | solution.py:202
  651.9 174.3 %copy-start.12 = (bf16[1280,64]{0,1:T(8,128)(2,1)S(1)}, bf16[1280,64]{0,1:T(8,128)(2,1)}, u32[]{:S(2)}) copy-start(bf16[1280,64]{0,1:T(8,128)(2,1)} %copy-done.11) | copy-start | bytes 491524
  827.4 105.3 %reduce-scatter.35.cloned.1.call-start = ((), (), s32[]{:S(2)}) async-start(), calls=%async_computation.24 | async-start | bytes 1105920 | tf_op jit(solution)/shard_map/reduce_scatter | solution.py:230
  832.4 101.9 %reduce-scatter.33.cloned.1.call-start = ((), (), s32[]{:S(2)}) async-start(), calls=%async_computation.23 | async-start | bytes 1105920 | tf_op jit(solution)/shard_map/reduce_scatter | solution.py:224
  836.9 114.7 %reduce-scatter.41.cloned.1.call-start = ((), (), s32[]{:S(2)}) async-start(), calls=%async_computation.27 | async-start | bytes 221184
  873.7 108.6 %reduce-scatter.39.cloned.1.call-start = ((), (), s32[]{:S(2)}) async-start(), calls=%async_computation.26 | async-start | bytes 368640
  876.1 138.0 %reduce-scatter.29.cloned.1.call-start = ((), (), s32[]{:S(2)}) async-start(), calls=%async_computation.21 | async-start | bytes 663552 | tf_op jit(solution)/shard_map/reduce_scatter | solution.py:221
  896.7 148.1 %reduce-scatter.37.cloned.1.call-start = ((), (), s32[]{:S(2)}) async-start(), calls=%async_computation.25 | async-start | bytes 368640
  901.3 176.4 %reduce-scatter.31.cloned.1.call-start = ((), (), s32[]{:S(2)}) async-start(), calls=%async_computation.22 | async-start | bytes 1105920 | tf_op jit(solution)/shard_map/reduce_scatter | solution.py:227
  905.9 395.4 %reduce-scatter.25.cloned.1.call-start = ((), (), s32[]{:S(2)}) async-start(), calls=%async_computation.19 | async-start | bytes 31457280 | tf_op jit(solution)/shard_map/reduce_scatter | solution.py:205
  931.9 369.4 %copy-start.19 = (f32[4,1024]{1,0:T(4,128)S(1)}, f32[4,1024]{1,0:T(4,128)}, u32[]{:S(2)}) copy-start(f32[4,1024]{1,0:T(4,128)} %copy-done.18) | copy-start | bytes 49156
  931.9 369.4 %copy-start.32 = (f32[768]{0:T(1024)S(1)}, f32[768]{0:T(1024)}, u32[]{:S(2)}) copy-start(f32[768]{0:T(1024)} %param.25) | copy-start | bytes 9220
  1079.3 229.7 %copy-start.23 = (f32[4,1024]{1,0:T(4,128)S(1)}, f32[4,1024]{1,0:T(4,128)}, u32[]{:S(2)}) copy-start(f32[4,1024]{1,0:T(4,128)} %copy-done.22) | copy-start | bytes 49156
  1079.3 229.8 %copy-start.21 = (f32[4,1024]{1,0:T(4,128)S(1)}, f32[4,1024]{1,0:T(4,128)}, u32[]{:S(2)}) copy-start(f32[4,1024]{1,0:T(4,128)} %copy-done.20) | copy-start | bytes 49156
  (46 other events, 785.7 us)
Sparse Core Ops, SparseCore 0:
  19.4 235.3 all-gather.7
  343.6 61.4 reduce-scatter.18
  408.5 39.6 all-gather.9
  449.8 39.6 all-gather.11
  499.3 61.4 reduce-scatter.22
  563.6 39.5 reduce-scatter.20
  608.3 39.6 all-gather.13
  827.5 25.3 reduce-scatter.26
  855.4 32.2 reduce-scatter.34
  889.8 30.2 reduce-scatter.32
  923.0 28.5 reduce-scatter.40
  953.7 28.5 reduce-scatter.38
  984.7 29.2 reduce-scatter.28
  1016.2 28.5 reduce-scatter.36
  1047.5 30.1 reduce-scatter.30
  1081.0 220.2 reduce-scatter.24
where the time goes:
time: 1390 us; the launch traced here: 1380 us
  waiting for transfers between devices  730 us (53%)
  matrix products  319 us (23%)
  blocking collectives  171 us (12%)
  other arithmetic  83.7 us (6%)
  local copies, waits for them, and re-layouts  58.1 us (4%)
  between operations  14.9 us (1%)
    reduce_scatter x1, waiting for transfers between devices, on_device(): lax.psum_scatter(byte_term.astype(jnp.bfloat16), 'tensor', scatter_dimens...  222 us
    all_gather x1, waiting for transfers between devices, on_device(): lax.all_gather(byte_norm, 'tensor', axis=1, tiled=True)  138 us
    unnamed x19, waiting for transfers between devices  74.4 us
    reduce_scatter x1, waiting for transfers between devices, on_device(): lax.psum_scatter(attn_term, 'tensor', scatter_dimension=1, tiled=True)  61.5 us
    reduce_scatter x1, waiting for transfers between devices, on_device(): lax.psum_scatter(hidden_term, 'tensor', scatter_dimension=1, tiled=True)  57 us
    dot_general x4, matrix products, score_backward(): jnp.einsum('hnl,nhd->lhd', grad_scores, query_heads, preferred_element_ty...  51.9 us
    dot_general x4, matrix products, score_backward(): jnp.einsum('hnl,lhd->nhd', grad_scores, key_heads, preferred_element_type...  50.9 us
    psum x1, blocking collectives, on_device(): lax.psum((grad_g_in, grad_b_in, grad_g_lat, grad_b_lat, grad_g_mlp, grad_...  40.9 us
  transfers between devices with their start and end apart: 16, of which 13 were waited for; matrix products, arithmetic and copies ran while one was open for 10% of the time, Pallas kernels for 0%

commit v1 on v0

--- a/solution.py
+++ b/solution.py
@@ -7,6 +7,28 @@
 HQ = 32
 HV = 160
 NEGATIVE = -1e30
+
+
+def laid_out(blocks, dim):
+    lengths = list(blocks.shape[1:])
+    lengths[dim] *= blocks.shape[0]
+    return jnp.moveaxis(blocks, 0, dim).reshape(lengths)
+
+
+def ring_gather(x, axis, dim):
+    length = lax.axis_size(axis)
+    pairs = [(i, (i + 1) % length) for i in range(length)]
+    back = [(b, a) for a, b in pairs]
+    lower, upper = ([], [])
+    for hop in range(length - 1):
+        if hop % 2 == 0:
+            lower.append(lax.ppermute(lower[-1] if lower else x, axis, pairs))
+        else:
+            upper.append(lax.ppermute(upper[-1] if upper else x, axis, back))
+    blocks = jnp.stack([*lower[::-1], x, *upper])
+    shift = lax.axis_index(axis) - len(lower)
+    blocks = blocks[(jnp.arange(length) - shift) % length]
+    return laid_out(blocks, dim)
 
 
 def normalize(values, gain, shift):
@@ -122,7 +144,7 @@
     byte_norm = normalize(byte_float, g_in, b_in).astype(jnp.bfloat16)
     latent_all, byte_all = (
         lax.all_gather(latent_norm, "tensor", axis=0, tiled=True),
-        lax.all_gather(byte_norm, "tensor", axis=1, tiled=True),
+        ring_gather(byte_norm, "tensor", 1),
     )
     keys = jnp.einsum("slc,cq->slq", byte_all, full_key, preferred_element_type=jnp.float32).astype(
         jnp.bfloat16

time: 1390 us -> 1710 us (1.23)
  blocking collectives: 171 us -> 381 us
  local copies, waits for them, and re-layouts: 58.1 us -> 121 us
  other arithmetic: 83.7 us -> 126 us
    all_gather x1, blocking collectives: 17.8 us -> 229 us  [on_device(): lax.all_gather(latent_norm, 'tensor', axis=0, tiled=True)]
    all_gather x1 -> x0, waiting for transfers between devices: 138 us -> none  [on_device(): lax.all_gather(byte_norm, 'tensor', axis=1, tiled=True)]
    ppermute x0 -> x3, waiting for transfers between devices: none -> 137 us  [the longest x2 137 us: ring_gather(): lower.append(lax.ppermute(lower[-1] if lower else x, axis, pairs))]
    gather x0 -> x5, local copies, waits for them, and re-layouts: none -> 43.5 us  [ring_gather(): blocks = blocks[(jnp.arange(length) - shift) % length]]
    another operation x0 -> x2, other arithmetic: none -> 23.6 us  [ring_gather(): blocks = jnp.stack([*lower[::-1], x, *upper])]
    transpose x0 -> x1, local copies, waits for them, and re-layouts: none -> 20.8 us  [laid_out(): return jnp.moveaxis(blocks, 0, dim).reshape(lengths)]
    transpose x0 -> x1, other arithmetic: none -> 17.7 us  [laid_out(): return jnp.moveaxis(blocks, 0, dim).reshape(lengths)]
    unnamed x19 -> x18, waiting for transfers between devices: 74.4 us -> 75.5 us
  transfers between devices with their start and end apart: 16 -> 18, of which waited for: 13 -> 13; matrix products, arithmetic and copies ran while one was open for 10% -> 8% of each run, Pallas kernels for 0% -> 0%
where the time goes in v1:
time: 1710 us; the launch traced here: 1700 us
  waiting for transfers between devices  731 us (43%)
  blocking collectives  381 us (22%)
  matrix products  319 us (19%)
  other arithmetic  126 us (7%)
  local copies, waits for them, and re-layouts  121 us (7%)
    all_gather x1, blocking collectives, on_device(): lax.all_gather(latent_norm, 'tensor', axis=0, tiled=True)  229 us
    reduce_scatter x1, waiting for transfers between devices, on_device(): lax.psum_scatter(byte_term.astype(jnp.bfloat16), 'tensor', scatter_dimens...  222 us
    ppermute x2, waiting for transfers between devices, ring_gather(): lower.append(lax.ppermute(lower[-1] if lower else x, axis, pairs))  137 us
    unnamed x18, waiting for transfers between devices  75.5 us
    reduce_scatter x1, waiting for transfers between devices, on_device(): lax.psum_scatter(attn_term, 'tensor', scatter_dimension=1, tiled=True)  62.3 us
    reduce_scatter x1, waiting for transfers between devices, on_device(): lax.psum_scatter(hidden_term, 'tensor', scatter_dimension=1, tiled=True)  57 us
    dot_general x4, matrix products, score_backward(): jnp.einsum('hnl,nhd->lhd', grad_scores, query_heads, preferred_element_ty...  51.9 us
    dot_general x4, matrix products, score_backward(): jnp.einsum('hnl,lhd->nhd', grad_scores, key_heads, preferred_element_type...  50.9 us
  transfers between devices with their start and end apart: 18, of which 13 were waited for; matrix products, arithmetic and copies ran while one was open for 8% of the time, Pallas kernels for 0%

profile of v1, /device:TPU:0, one launch (start us, length us, event | category | flops | bytes accessed | tf_op | source)
XLA Modules:
  0.0 1699.7 jit_solution(10432254371810510722)
XLA Ops:
  22.1 136.6 %collective-permute-done = bf16[4,1024,768]{2,1,0:T(8,128)(2,1)} collective-permute-done((bf16[4,1024,768]{2,1,0:T(8,128)(2,1)}, bf16[4,1024,768]{2,1,0:T(8,128)(2,1)}, u32[]{:S(2)}, u32[]{:S(2)}) %collective-permute-start) | collective-permute-done | bytes 6291488 | tf_op jit(solution)/shard_map/ppermute | solution.py:25
  204.2 229.4 %all_gather.36 = bf16[256,1280]{1,0:T(8,128)(2,1)S(1)} all-gather(bf16[64,1280]{1,0:T(8,128)(2,1)S(1)} %add_convert_fusion.4), channel_id=1, replica_groups=mesh['dp'=8,'tensor'=4] {'tensor'}, dimensions={0}, use_global_device_ids=true | all-gather | bytes 819200 | tf_op jit(solution)/shard_map/all_gather | solution.py:146
  449.2 17.9 %all_gather.38 = bf16[320,1280]{0,1:T(8,128)(2,1)} all-gather(bf16[320,160]{0,1:T(8,128)(2,1)S(1)} %copy-done.28), channel_id=1, replica_groups=mesh['dp'=8,'tensor'=4] {'dp'}, dimensions={1}, use_global_device_ids=true | all-gather | bytes 921600 | tf_op jit(solution)/shard_map/all_gather | solution.py:136
  472.0 18.7 %pad_maximum_fusion = bf16[4,4,1024,768]{3,2,1,0:T(8,128)(2,1)} fusion(bf16[1,4,1024,768]{3,2,1,0:T(8,128)(2,1)} %bitcast.27, bf16[1,4,1024,768]{3,2,1,0:T(8,128)(2,1)S(1)} %fusion.114, bf16[1,4,1024,768]{3,2,1,0:T(8,128)(2,1)} %bitcast.25, bf16[1,4,1024,768]{3,2,1,0:T(8,128)(2,1)} %bitcast.24), kind=kLoop, calls=%fused_computation.43 | loop fusion | flops 37748736 | bytes 50331648 | tf_op jit(solution)/shard_map/stack | solution.py:28
  490.7 18.1 %fusion.68 = (bf16[4,4,256,768]{3,2,1,0:T(8,128)(2,1)}, bf16[4,4,256,768]{3,2,1,0:T(8,128)(2,1)}, bf16[4,4,256,768]{3,2,1,0:T(8,128)(2,1)}, bf16[4,4,256,768]{3,2,1,0:T(8,128)(2,1)}) fusion(bf16[4,4,1024,768]{3,2,1,0:T(8,128)(2,1)} %pad_maximum_fusion), kind=kLoop, calls=%fused_computation.166 | loop fusion | bytes 50331648 | tf_op jit(solution)/shard_map/gather | solution.py:30
  534.2 17.7 %maximum_bitcast_fusion = bf16[4,4,1024,768]{3,2,0,1:T(8,128)(2,1)} fusion(bf16[4,4,256,768]{3,2,1,0:T(8,128)(2,1)} %gather_fusion.3, bf16[4,4,256,768]{3,2,1,0:T(8,128)(2,1)} %gather_fusion.2, bf16[4,4,256,768]{3,2,1,0:T(8,128)(2,1)} %gather_fusion.1, bf16[4,4,256,768]{3,2,1,0:T(8,128)(2,1)} %gather_fusion), kind=kLoop, calls=%fused_computation.44 | loop fusion | flops 100663296 | bytes 50331648 | tf_op jit(solution)/shard_map/transpose | solution.py:15
  551.9 20.8 %copy.63 = bf16[4,4,1024,768]{3,2,1,0:T(8,128)(2,1)} copy(bf16[4,4,1024,768]{3,2,0,1:T(8,128)(2,1)} %maximum_bitcast_fusion) | data formatting | bytes 50331648 | tf_op jit(solution)/shard_map/transpose | solution.py:15
  605.5 50.5 %while.26 = (s32[]{:T(128)}, bf16[4,256,320]{1,2,0:T(8,128)(2,1)}, f32[4,2,256]{2,1,0:T(2,128)S(1)}, bf16[4,4096,320]{1,2,0:T(8,128)(2,1)}, s32[4]{0:T(128)S(1)}...) while((s32[]{:T(128)}, bf16[4,256,320]{1,2,0:T(8,128)(2,1)}, ...), condition=%wide.region_7.8_spmd, body=%wide.region_4.7_spmd.sunk | while | flops 830557696 | bytes 35160188 | solution.py:156
  661.6 62.3 %reduce-scatter.19.cloned.1.call-done = f32[4,64,1280]{2,1,0:T(8,128)} async-done(((f32[4,256,1280]{2,1,0:T(8,128)}), f32[4,64,1280]{2,1,0:T(8,128)}) %reduce-scatter.19.cloned.1.call-update) | async-done | bytes 1310736 | tf_op jit(solution)/shard_map/reduce_scatter | solution.py:158
  747.4 17.6 %all_gather.41 = bf16[320,1280]{0,1:T(8,128)(2,1)} all-gather(bf16[320,160]{0,1:T(8,128)(2,1)S(1)} %copy-done.30), channel_id=1, replica_groups=mesh['dp'=8,'tensor'=4] {'dp'}, dimensions={1}, use_global_device_ids=true | all-gather | bytes 921600 | tf_op jit(solution)/shard_map/all_gather | solution.py:137
  776.8 33.0 %all-gather.9.cloned.1.call-done = bf16[4,256,1280]{2,1,0:T(8,128)(2,1)} async-done(((bf16[4,64,1280]{2,1,0:T(8,128)(2,1)}), bf16[4,256,1280]{2,1,0:T(8,128)(2,1)}) %all-gather.9.cloned.1.call-update) | async-done | bytes 2621456 | tf_op jit(solution)/shard_map/all_gather | solution.py:164
  824.1 57.0 %reduce-scatter.23.cloned.1.call-done = f32[4,64,1280]{2,1,0:T(8,128)} async-done(((f32[4,256,1280]{2,1,0:T(8,128)}), f32[4,64,1280]{2,1,0:T(8,128)}) %reduce-scatter.23.cloned.1.call-update) | async-done | bytes 1310736 | tf_op jit(solution)/shard_map/reduce_scatter | solution.py:194
  883.4 40.0 %reduce-scatter.21.cloned.1.call-done = bf16[4,64,1280]{2,1,0:T(8,128)(2,1)} async-done(((bf16[4,256,1280]{2,1,0:T(8,128)(2,1)}), bf16[4,64,1280]{2,1,0:T(8,128)(2,1)}) %reduce-scatter.21.cloned.1.call-update) | async-done | bytes 655376 | tf_op jit(solution)/shard_map/reduce_scatter | solution.py:176
  928.6 39.7 %all-gather.11.cloned.1.call-done = bf16[4,256,1280]{2,1,0:T(8,128)(2,1)} async-done(((bf16[4,64,1280]{2,1,0:T(8,128)(2,1)}), bf16[4,256,1280]{2,1,0:T(8,128)(2,1)}) %all-gather.11.cloned.1.call-update) | async-done | bytes 2621456 | tf_op jit(solution)/shard_map/all_gather | solution.py:198
  972.2 174.4 %while.27 = (s32[]{:T(128)}, bf16[4,256,64]{1,2,0:T(8,128)(2,1)S(1)}, bf16[4,4096,64]{1,2,0:T(8,128)(2,1)S(1)}, bf16[4,4096,320]{1,2,0:T(8,128)(2,1)}, bf16[4,40...) while((s32[]{:T(128)}, ...), condition=%wide.region_17.18_spmd, body=%wide.region_15.17_spmd.sunk | while | flops 1772368896 | bytes 112507056 | solution.py:203
  1168.8 25.0 %fusion.47 = f32[4,4096,768]{2,1,0:T(8,128)} fusion(bf16[4,4096,320]{1,2,0:T(8,128)(2,1)} %get-tuple-element.112, bf16[768,320]{1,0:T(8,128)(2,1)S(1)} %copy-done.12), kind=kOutput, calls=%fused_computation.121 | convolution fusion | flops 8053063680 | bytes 61308928 | tf_op jit(solution)/shard_map/slv,cv->slc/dot_general | solution.py:220
  1196.5 20.4 %fusion.31 = bf16[768,320]{1,0:T(8,128)(2,1)} fusion(bf16[4,4096,768]{2,1,0:T(8,128)(2,1)} %bitcast.258, bf16[4,4096,320]{1,2,0:T(8,128)(2,1)} %get-tuple-element.112), kind=kOutput, calls=%fused_computation.80 | convolution fusion | flops 8053309440 | bytes 36143104 | tf_op jit(solution)/shard_map/slc,slv->cv/dot_general | solution.py:216
  1226.4 25.7 %add_convert_fusion = bf16[4,4096,768]{2,1,0:T(8,128)(2,1)} fusion(f32[4,4096,768]{2,1,0:T(8,128)} %fusion.47, bf16[4,4096,64]{1,2,0:T(8,128)(2,1)S(1)} %get-tuple-element.111, bf16[768,64,1]{0,1,2:T(8,128)(2,1)S(1)} %copy-done.18), kind=kOutput, calls=%fused_computation.42 | convolution fusion | flops 1635778560 | bytes 77692928 | tf_op jit(solution)/shard_map/slq,cq->slc/dot_general | solution.py:219
  1273.8 29.5 %reduce-scatter.39.cloned.1.call-done = bf16[160,64]{1,0:T(8,128)(2,1)} async-done(((bf16[1280,64]{1,0:T(8,128)(2,1)}), bf16[160,64]{1,0:T(8,128)(2,1)}) %reduce-scatter.39.cloned.1.call-update) | async-done | bytes 20496
  1304.8 30.1 %reduce-scatter.29.cloned.1.call-done = bf16[96,320]{1,0:T(8,128)(2,1)} async-done(((bf16[768,320]{1,0:T(8,128)(2,1)}), bf16[96,320]{1,0:T(8,128)(2,1)}) %reduce-scatter.29.cloned.1.call-update) | async-done | bytes 61456 | tf_op jit(solution)/shard_map/reduce_scatter | solution.py:243
  1336.4 29.5 %reduce-scatter.37.cloned.1.call-done = bf16[160,64]{1,0:T(8,128)(2,1)} async-done(((bf16[1280,64]{1,0:T(8,128)(2,1)}), bf16[160,64]{1,0:T(8,128)(2,1)}) %reduce-scatter.37.cloned.1.call-update) | async-done | bytes 20496
  1367.5 31.3 %reduce-scatter.31.cloned.1.call-done = bf16[320,160]{0,1:T(8,128)(2,1)} async-done(((bf16[320,1280]{0,1:T(8,128)(2,1)}), bf16[320,160]{0,1:T(8,128)(2,1)}) %reduce-scatter.31.cloned.1.call-update) | async-done | bytes 102416 | tf_op jit(solution)/shard_map/reduce_scatter | solution.py:249
  1400.4 221.9 %reduce-scatter.25.cloned.1.call-done = bf16[4,1024,768]{2,1,0:T(8,128)(2,1)} async-done(((bf16[4,4096,768]{2,1,0:T(8,128)(2,1)}), bf16[4,1024,768]{2,1,0:T(8,128)(2,1)}) %reduce-scatter.25.cloned.1.call-update) | async-done | bytes 6291472 | tf_op jit(solution)/shard_map/reduce_scatter | solution.py:227
  1639.3 40.9 %all-reduce = (f32[768]{0:T(1024)}, f32[768]{0:T(1024)}, f32[1280]{0:T(1024)}, f32[1280]{0:T(1024)}, f32[1280]{0:T(1024)}, /*index=5*/f32[1280]{0:T(1024)}, f32[1280]{0:T(1024)}, f32[1280]{0:T(1024)}) all-reduce(f32[768]{0:T(1024)S(1)} %get-tuple-element.114, ...), channel_id=1, replica_groups=mesh['dp'=8,'tensor'=4] {'dp','tensor'}, use_global_device_ids=true, to_apply=%region_28.29 | all-reduce | flops 9216 | bytes 73728 | tf_op jit(solution)/shard_map/psum | solution.py:272
  (327 shorter events, 520.7 us)
Async XLA Ops:
  7.2 716.7 %reduce-scatter.19.cloned.1.call-start = ((), (), s32[]{:S(2)}) async-start(), calls=%async_computation.12 | async-start | bytes 6553600 | tf_op jit(solution)/shard_map/reduce_scatter | solution.py:158
  11.8 455.2 %copy-start.19 = (f32[4,1024]{1,0:T(4,128)}, f32[4,1024]{1,0:T(4,128)S(1)}, u32[]{:S(2)}) copy-start(f32[4,1024]{1,0:T(4,128)S(1)} %broadcast_multiply_fusion) | copy-start | bytes 49156
  13.8 453.3 %copy-start.22 = (f32[4,1024]{1,0:T(4,128)}, f32[4,1024]{1,0:T(4,128)S(1)}, u32[]{:S(2)}) copy-start(f32[4,1024]{1,0:T(4,128)S(1)} %fusion.58) | copy-start | bytes 49156
  18.2 140.5 %collective-permute-start = (bf16[4,1024,768]{2,1,0:T(8,128)(2,1)}, bf16[4,1024,768]{2,1,0:T(8,128)(2,1)}, u32[]{:S(2)}, u32[]{:S(2)}) collective-permute-start(bf16[4,1024,768]{2,1,0:T(8,128)(2,1)} %fusion.22), channel_id=1, source_target_pairs={{0,1},{1,2},{2,3},{3,0},{4,5},{5,6},{6,7},{7,4},{8,9},{9,10},{10,1... | collective-permute-start | bytes 18874376 | tf_op jit(solution)/shard_map/ppermute | solution.py:25
  21.1 450.9 %collective-permute-start.2 = (bf16[4,1024,768]{2,1,0:T(8,128)(2,1)}, bf16[4,1024,768]{2,1,0:T(8,128)(2,1)}, u32[]{:S(2)}, u32[]{:S(2)}) collective-permute-start(bf16[4,1024,768]{2,1,0:T(8,128)(2,1)} %fusion.22), channel_id=1, source_target_pairs={{1,0},{2,1},{3,2},{0,3},{5,4},{6,5},{7,6},{4,7},{9,8},{10,9},{11,1... | collective-permute-start | bytes 18874376 | tf_op jit(solution)/shard_map/ppermute | solution.py:27
  158.7 313.3 %collective-permute-start.1 = (bf16[4,1024,768]{2,1,0:T(8,128)(2,1)}, bf16[4,1024,768]{2,1,0:T(8,128)(2,1)}, u32[]{:S(2)}, u32[]{:S(2)}) collective-permute-start(bf16[4,1024,768]{2,1,0:T(8,128)(2,1)} %collective-permute-done), channel_id=1, source_target_pairs={{0,1},{1,2},{2,3},{3,0},{4,5},{5,6},{6,7},{7,4},{8,9},{9,10},{10,1... | collective-permute-start | bytes 18874376 | tf_op jit(solution)/shard_map/ppermute | solution.py:25
  174.3 398.4 %copy-start.17 = (bf16[768,64,1]{0,1,2:T(8,128)(2,1)}, bf16[768,64,1]{0,1,2:T(8,128)(2,1)S(1)}, u32[]{:S(2)}) copy-start(bf16[768,64,1]{0,1,2:T(8,128)(2,1)S(1)} %reshape.326) | copy-start | bytes 294916
  188.9 278.1 %copy-start.3 = (f32[1280,64]{0,1:T(8,128)}, f32[1280,64]{0,1:T(8,128)S(1)}, u32[]{:S(2)}) copy-start(f32[1280,64]{0,1:T(8,128)S(1)} %reshape.324) | copy-start | bytes 983044
  661.5 106.7 %all-gather.7.cloned.1.call-start = ((), (), s32[]{:S(2)}) async-start(), calls=%async_computation.13 | async-start | bytes 3276800 | tf_op jit(solution)/shard_map/all_gather | solution.py:163
  728.5 81.3 %all-gather.9.cloned.1.call-start = ((), (), s32[]{:S(2)}) async-start(), calls=%async_computation.15 | async-start | bytes 3276800 | tf_op jit(solution)/shard_map/all_gather | solution.py:164
  729.4 151.6 %reduce-scatter.23.cloned.1.call-start = ((), (), s32[]{:S(2)}) async-start(), calls=%async_computation.16 | async-start | bytes 6553600 | tf_op jit(solution)/shard_map/reduce_scatter | solution.py:194
  819.5 104.0 %reduce-scatter.21.cloned.1.call-start = ((), (), s32[]{:S(2)}) async-start(), calls=%async_computation.14 | async-start | bytes 3276800 | tf_op jit(solution)/shard_map/reduce_scatter | solution.py:176
  824.0 144.3 %all-gather.11.cloned.1.call-start = ((), (), s32[]{:S(2)}) async-start(), calls=%async_computation.17 | async-start | bytes 3276800 | tf_op jit(solution)/shard_map/all_gather | solution.py:198
  928.5 288.6 %reduce-scatter.27.cloned.1.call-start = ((), (), s32[]{:S(2)}) async-start(), calls=%async_computation.19 | async-start | bytes 819200 | tf_op jit(solution)/shard_map/reduce_scatter | solution.py:224
  1147.9 105.0 %reduce-scatter.35.cloned.1.call-start = ((), (), s32[]{:S(2)}) async-start(), calls=%async_computation.23 | async-start | bytes 1105920 | tf_op jit(solution)/shard_map/reduce_scatter | solution.py:252
  1152.7 101.9 %reduce-scatter.33.cloned.1.call-start = ((), (), s32[]{:S(2)}) async-start(), calls=%async_computation.22 | async-start | bytes 1105920 | tf_op jit(solution)/shard_map/reduce_scatter | solution.py:246
  1157.2 115.2 %reduce-scatter.41.cloned.1.call-start = ((), (), s32[]{:S(2)}) async-start(), calls=%async_computation.26 | async-start | bytes 221184
  1193.9 109.4 %reduce-scatter.39.cloned.1.call-start = ((), (), s32[]{:S(2)}) async-start(), calls=%async_computation.25 | async-start | bytes 368640
  1196.3 138.6 %reduce-scatter.29.cloned.1.call-start = ((), (), s32[]{:S(2)}) async-start(), calls=%async_computation.20 | async-start | bytes 663552 | tf_op jit(solution)/shard_map/reduce_scatter | solution.py:243
  1217.0 149.0 %reduce-scatter.37.cloned.1.call-start = ((), (), s32[]{:S(2)}) async-start(), calls=%async_computation.24 | async-start | bytes 368640
  1221.5 177.2 %reduce-scatter.31.cloned.1.call-start = ((), (), s32[]{:S(2)}) async-start(), calls=%async_computation.21 | async-start | bytes 1105920 | tf_op jit(solution)/shard_map/reduce_scatter | solution.py:249
  1226.1 396.2 %reduce-scatter.25.cloned.1.call-start = ((), (), s32[]{:S(2)}) async-start(), calls=%async_computation.18 | async-start | bytes 31457280 | tf_op jit(solution)/shard_map/reduce_scatter | solution.py:227
  1252.1 370.2 %copy-start.20 = (f32[4,1024]{1,0:T(4,128)S(1)}, f32[4,1024]{1,0:T(4,128)}, u32[]{:S(2)}) copy-start(f32[4,1024]{1,0:T(4,128)} %copy-done.19) | copy-start | bytes 49156
  1252.1 370.2 %copy-start.32 = (f32[768]{0:T(1024)S(1)}, f32[768]{0:T(1024)}, u32[]{:S(2)}) copy-start(f32[768]{0:T(1024)} %param.25) | copy-start | bytes 9220
  (50 other events, 3824.5 us)
Sparse Core Ops, SparseCore 0:
  661.6 62.2 reduce-scatter.18
  728.6 39.6 all-gather.6
  770.1 39.6 all-gather.8
  819.6 61.4 reduce-scatter.22
  883.9 39.5 reduce-scatter.20
  928.6 39.6 all-gather.10
  1148.0 25.3 reduce-scatter.26
  1175.9 31.9 reduce-scatter.34
  1210.2 30.5 reduce-scatter.32
  1243.5 28.7 reduce-scatter.40
  1274.6 28.6 reduce-scatter.38
  1305.5 29.2 reduce-scatter.28
  1337.2 28.6 reduce-scatter.36
  1368.7 30.0 reduce-scatter.30
  1402.0 220.2 reduce-scatter.24
